TPU v7x, 256 devices: a whole 4x4x8 slice. The times are simulated.
256 devices in a mesh: lat: 8 (over y, z_hi), lon: 32 (over x, z_lo, core).
Axes of the slice: x: 4, y: 4, z: 8 (z_hi: 2, z_lo: 4; z = z_hi * 4 + z_lo), core: 2. Of those that a mesh axis runs over, the one named last changes fastest.
Arguments:
- sea_level: float32 [4096, 1024], P('lon', 'lat'), may hold values from -1 to 5
- east_velocity: float32 [4096, 1024], P('lon', 'lat'), may hold values from -6 to 6
- north_velocity: float32 [4096, 1024], P('lon', 'lat'), may hold values from -6 to 6
- depth: float32 [4096, 1024], P('lon', 'lat'), may hold values from 0.25 to 1
- land_mask: int32 [4096, 1024], P('lon', 'lat'), may hold values from 0 to 1, as said below
- wet_counts: int32 [8, 32], replicated, may hold values from 1 to 16384, as said below
- loading_prev: float32 [4096, 1024], P('lon', 'lat'), may hold values from -4 to 4
- tide_amp: float32 [8], replicated, may hold values from 0.3 to 1
- tide_phase: float32 [8], replicated, may hold values from -3.140625 to 3.140625
- legendre: bfloat16 [1024, 1024, 1024], P('lon', None, 'lat'), may hold values from -0.1875 to 0.1875
- love_factor: float32 [1024], replicated, may hold values from 0.05 to 1
Outputs:
- height_new: float32 [4096, 1024], P('lon', 'lat')
- east_new: float32 [4096, 1024], P('lon', 'lat')
- north_new: float32 [4096, 1024], P('lon', 'lat')
- self_attraction: float32 [4096, 1024], P('lon', 'lat')
Inputs may be any that keep to these rules, and one draw needn't show every extreme that they name: `land_mask`: every tile of 128 columns by 128 rows holds at least one wet column, and one tile is wholly wet. wet_counts[p, q] is the number of wet columns of land_mask in latitude band p and longitude band q.
All inputs are finite; a program needn't handle non-finite values.
Results may differ from a plain program's by a relative error of at most 0.0038.
Values may be sent and summed in bfloat16 or wider, within the bound.
A program may use at most 64 MiB of HBM per device.

v0:
```python
import math
import jax
import jax.numpy as jnp
from jax import lax
from jax.sharding import Mesh
from jax.sharding import PartitionSpec as P

SUBSTEPS = 4
LON = ("lon_0", "lon_1", "lon_2")
LAT = ("lat_0", "lat_1")
LAT_LON = ("lat_0", "lat_1", "lon_0", "lon_1", "lon_2")
lat_edge = 1.3089969
courant = 0.4
friction = 0.02
rotation = 0.2
frequencies = (0.1405, 0.1454, 0.1379, 0.1458, 0.0729, 0.0676, 0.0725, 0.0649)
orders = (2, 2, 2, 2, 1, 1, 1, 1)
highest = lax.Precision.HIGHEST


def padded(cells, sides, width, closed):
    for axis, dim in sides:
        count = lax.axis_size(axis)
        ends = count if closed else count - 1
        head = lax.slice_in_dim(cells, 0, width, axis=dim)
        tail = lax.slice_in_dim(cells, cells.shape[dim] - width, cells.shape[dim], axis=dim)
        cells = jnp.concatenate(
            [
                lax.ppermute(tail, axis, [(i, (i + 1) % count) for i in range(ends)]),
                cells,
                lax.ppermute(head, axis, [((i + 1) % count, i) for i in range(ends)]),
            ],
            axis=dim,
        )
    return cells


def one_axis_at_a_time(value, axes):
    for axis in axes:
        value = lax.psum(value, axis)
    return value


def in_blocks(value, dim, size):
    before, after = (value.shape[:dim], value.shape[dim + 1 :])
    return jnp.moveaxis(value.reshape(*before, size, -1, *after), dim, 0)


def sum_at_owner(value, axis, dim):
    size = lax.axis_size(axis)
    tiles = lax.all_to_all(in_blocks(value, dim, size), axis, 0, 0, tiled=True)
    return jnp.sum(tiles, axis=0)


def from_everyone(value, axis):
    copies = jnp.broadcast_to(value, (lax.axis_size(axis), *value.shape))
    return lax.all_to_all(copies, axis, split_axis=0, concat_axis=0, tiled=True)


def of_everyone(value, axis):
    return from_everyone(value, axis).sum(axis=0)


def latitude_of(rows, total_rows):
    return -lat_edge + 2.0 * lat_edge * (rows.astype(jnp.float32) + 0.5) / total_rows


def potential(columns, rows, moment, total_cols, total_rows, tide_amp, tide_phase):
    longitude = (2.0 * math.pi * (columns % total_cols).astype(jnp.float32) / total_cols)[:, None]
    latitude = latitude_of(rows, total_rows)[None, :]
    semi = jnp.cos(latitude) ** 2
    diurnal = jnp.sin(2.0 * latitude)
    field = jnp.zeros((columns.shape[0], rows.shape[0]), jnp.float32)
    for index in range(len(frequencies)):
        shape_term = semi if orders[index] == 2 else diurnal
        field = field + tide_amp[index] * shape_term * jnp.cos(
            frequencies[index] * moment + orders[index] * longitude + tide_phase[index]
        )
    return field * (total_cols / 64.0)


def advance(state_x, static_x, forcing, latitude_x):
    height_x, east_x, north_x = (state_x[0], state_x[1], state_x[2])
    depth_x, wet_x, loading_x = (static_x[0], static_x[1], static_x[2])
    cosine = jnp.cos(latitude_x)[None, :]
    secant_cycle = (1.0 / jnp.cos(latitude_x[1:-1]))[None, :]
    secant_core = (1.0 / jnp.cos(latitude_x[2:-2]))[None, :]
    coriolis = (rotation * jnp.sin(latitude_x[2:-2]))[None, :]
    flux_east = depth_x * east_x
    flux_north = depth_x * north_x * cosine
    divergence = (
        (
            flux_east[2:, 1:-1]
            - flux_east[:-2, 1:-1]
            + (flux_north[1:-1, 2:] - flux_north[1:-1, :-2])
        )
        * 0.5
        * secant_cycle
    )
    height_cycle = height_x[1:-1, 1:-1] - courant * divergence * wet_x[1:-1, 1:-1]
    pressure = height_cycle - forcing - loading_x[1:-1, 1:-1]
    slope_east = (pressure[2:, 1:-1] - pressure[:-2, 1:-1]) * 0.5 * secant_core
    slope_north = (pressure[1:-1, 2:] - pressure[1:-1, :-2]) * 0.5
    east = east_x[2:-2, 2:-2]
    north = north_x[2:-2, 2:-2]
    wet = wet_x[2:-2, 2:-2]
    east_next = wet * ((1.0 - friction) * east + courant * (coriolis * north - slope_east))
    north_next = wet * ((1.0 - friction) * north - courant * (coriolis * east + slope_north))
    return jnp.stack([height_cycle[1:-1, 1:-1], east_next, north_next])


def extend_margin(fields, margin):
    wide = padded(fields, ((LON, 1),), margin, True)
    return padded(wide, ((LAT, 2),), margin, False)


def wave_table(waves, columns, total_cols, weights):
    turns = waves[None, :] * columns[:, None] % total_cols
    angle = 2.0 * math.pi * turns.astype(jnp.float32) / total_cols
    scale = weights[None, :] / math.sqrt(total_cols)
    return jnp.stack([scale * jnp.cos(angle), -scale * jnp.sin(angle)], axis=2)


def shards(
    sea_level,
    east_velocity,
    north_velocity,
    depth,
    land_mask,
    wet_counts,
    loading_prev,
    tide_amp,
    tide_phase,
    legendre,
    love_factor,
):
    lon_dev, lat_dev = sea_level.shape
    wave_dev = legendre.shape[0]
    lon_count = lax.axis_size(LON)
    total_cols = lon_dev * lon_count
    total_rows = lat_dev * lax.axis_size(LAT)
    lon_index = lax.axis_index(LON)
    lon_start = lon_index * lon_dev
    lat_start = lax.axis_index(LAT) * lat_dev
    wet = land_mask.astype(jnp.float32)
    margin = 2 * SUBSTEPS
    full = extend_margin(
        jnp.stack([sea_level, east_velocity, north_velocity, depth, wet, loading_prev]), margin
    )
    state_x = full[:3]
    static_full = full[3:]
    wide_cols = full.shape[1]
    wide_rows = full.shape[2]
    for moment in range(SUBSTEPS):
        reach = margin - 2 * moment
        offset = margin - reach
        static_x = static_full[:, offset : wide_cols - offset, offset : wide_rows - offset]
        latitude_x = jnp.clip(
            latitude_of(
                lat_start + jnp.arange(-reach, lat_dev + reach, dtype=jnp.int32), total_rows
            ),
            -1.5,
            1.5,
        )
        columns = lon_start + jnp.arange(1 - reach, lon_dev + reach - 1, dtype=jnp.int32)
        rows = lat_start + jnp.arange(1 - reach, lat_dev + reach - 1, dtype=jnp.int32)
        forcing = potential(
            columns, rows, float(moment), total_cols, total_rows, tide_amp, tide_phase
        )
        state_x = advance(state_x, static_x, forcing, latitude_x)
    height = state_x[0]
    wet_sum = one_axis_at_a_time(jnp.sum(wet * height), LAT_LON)
    mean_level = wet_sum / jnp.sum(wet_counts.astype(jnp.float32))
    anomaly = wet * (height - mean_level)
    local_cols = lon_start + jnp.arange(lon_dev, dtype=jnp.int32)
    count = wave_dev * lax.axis_size(LON)
    waves = jnp.arange(count, dtype=jnp.int32)
    table = wave_table(waves, local_cols, total_cols, jnp.ones((count,), jnp.float32))
    table = jnp.transpose(table, (1, 2, 0)).reshape(2 * count, lon_dev)
    fourier = sum_at_owner(
        jnp.dot(table, anomaly, precision=highest, preferred_element_type=jnp.float32).reshape(
            count, 2, lat_dev
        ),
        LON,
        0,
    ).astype(jnp.bfloat16)
    coefficients = lax.dot_general(
        fourier, legendre, (((2,), (2,)), ((0,), (0,))), preferred_element_type=jnp.float32
    )
    coefficients = of_everyone(coefficients, LAT)
    scaled = (coefficients * love_factor[None, None, :]).astype(jnp.bfloat16)
    synthesis = lax.dot_general(
        scaled, legendre, (((2,), (1,)), ((0,), (0,))), preferred_element_type=jnp.float32
    )
    own_waves = lon_index * wave_dev + jnp.arange(wave_dev, dtype=jnp.int32)
    weights = jnp.where(own_waves == 0, 1.0, 2.0).astype(jnp.float32)
    flat_spectra = synthesis.reshape(2 * wave_dev, lat_dev)
    count = lon_dev * lax.axis_size(LON)
    cells = jnp.arange(count, dtype=jnp.int32)
    table = wave_table(own_waves, cells, total_cols, weights).reshape(count, 2 * wave_dev)
    self_attraction = sum_at_owner(
        jnp.dot(table, flat_spectra, precision=highest, preferred_element_type=jnp.float32), LON, 0
    )
    return (state_x[0], state_x[1], state_x[2], self_attraction)


def solution(mesh):
    torus = Mesh(mesh.devices.reshape(4, 2, 4, 4, 2), ("lat_0", "lat_1", "lon_0", "lon_1", "lon_2"))
    return jax.shard_map(
        shards,
        mesh=torus,
        in_specs=(
            P(LON, LAT),
            P(LON, LAT),
            P(LON, LAT),
            P(LON, LAT),
            P(LON, LAT),
            P(),
            P(LON, LAT),
            P(),
            P(),
            P(LON, None, LAT),
            P(),
        ),
        out_specs=(P(LON, LAT), P(LON, LAT), P(LON, LAT), P(LON, LAT)),
        check_vma=False,
    )
```

profile of v0, /device:TPU:1, one launch (start us, length us, event | category | flops | bytes accessed | tf_op | source)
XLA Modules:
  0.0 320.3 jit_solution(9844729480353911763)
XLA Ops:
  5.7 3.3 %collective-permute-start.1 = (f32[6,8,128]{2,1,0:T(8,128)S(1)}, f32[6,8,128]{2,1,0:T(8,128)S(1)}, u32[]{:S(2)}, u32[]{:S(2)}) collective-permute-start(f32[6,8,128]{2,1,0:T(8,128)S(1)} %get-tuple-element.50), channel_id=1, source_target_pairs={{1,0},{2,1},{3,2},{4,3},{5,4},{6,5},{7,6},{8,7},{9,8},{10,9},{11,1... | collective-permute-start | bytes 73736 | tf_op jit(solution)/shard_map/ppermute | solution.py:31
  9.1 1.6 fusion.112
  13.2 1.6 fusion.111
  56.6 8.8 %collective-permute-start.2 = (f32[6,144,8]{2,1,0:T(8,128)S(1)}, f32[6,144,8]{2,1,0:T(8,128)S(1)}, u32[]{:S(2)}, u32[]{:S(2)}) collective-permute-start(f32[6,144,8]{2,1,0:T(8,128)S(1)} %get-tuple-element.47), channel_id=1, source_target_pairs={{0,32},{32,64},{64,96},{96,128},{128,160},{160,192},{192,224},{1,3... | collective-permute-start | bytes 82952 | tf_op jit(solution)/shard_map/ppermute | solution.py:29
  65.4 4.6 %collective-permute-done.3 = f32[6,144,8]{2,1,0:T(8,128)S(1)} collective-permute-done((f32[6,144,8]{2,1,0:T(8,128)S(1)}, f32[6,144,8]{2,1,0:T(8,128)S(1)}, u32[]{:S(2)}, u32[]{:S(2)}) %collective-permute-start.3) | collective-permute-done | bytes 27680 | tf_op jit(solution)/shard_map/ppermute | solution.py:31
  76.6 27.8 %psum.35 = f32[]{:T(128)} all-reduce(f32[]{:T(128)} %get-tuple-element.4), channel_id=1, replica_groups=mesh['lat_0'=4,'lat_1'=2,'lon_0'=4,'lon_1'=4,'lon_2'=2] {'lat_0'}, use_global_device_ids=true, to_apply=%region_1.2 | all-reduce | flops 1 | bytes 8 | tf_op jit(solution)/shard_map/psum | solution.py:40
  104.4 2.1 cosine_multiply_fusion
  106.6 8.6 %psum.36 = f32[]{:T(128)} all-reduce(f32[]{:T(128)} %psum.35), channel_id=1, replica_groups=mesh['lat_0'=4,'lat_1'=2,'lon_0'=4,'lon_1'=4,'lon_2'=2] {'lat_1'}, use_global_device_ids=true, to_apply=%region_2.3 | all-reduce | flops 1 | bytes 8 | tf_op jit(solution)/shard_map/psum | solution.py:40
  115.3 11.1 %psum.37 = f32[]{:T(128)} all-reduce(f32[]{:T(128)} %psum.36), channel_id=1, replica_groups=mesh['lat_0'=4,'lat_1'=2,'lon_0'=4,'lon_1'=4,'lon_2'=2] {'lon_0'}, use_global_device_ids=true, to_apply=%region_3.4 | all-reduce | flops 1 | bytes 8 | tf_op jit(solution)/shard_map/psum | solution.py:40
  127.0 18.4 %psum.38 = f32[]{:T(128)} all-reduce(f32[]{:T(128)} %psum.37), channel_id=1, replica_groups=mesh['lat_0'=4,'lat_1'=2,'lon_0'=4,'lon_1'=4,'lon_2'=2] {'lon_1'}, use_global_device_ids=true, to_apply=%region_4.5 | all-reduce | flops 1 | bytes 8 | tf_op jit(solution)/shard_map/psum | solution.py:40
  145.7 10.4 %psum.39 = f32[]{:T(128)} all-reduce(f32[]{:T(128)} %psum.38), channel_id=1, replica_groups=mesh['lat_0'=4,'lat_1'=2,'lon_0'=4,'lon_1'=4,'lon_2'=2] {'lon_2'}, use_global_device_ids=true, to_apply=%region_5.6 | all-reduce | flops 1 | bytes 8 | tf_op jit(solution)/shard_map/psum | solution.py:40
  158.4 31.0 %all_to_all.15 = f32[32,32,2,128]{3,1,2,0:T(8,128)S(1)} all-to-all(f32[32,32,2,128]{3,1,2,0:T(8,128)S(1)} %fusion.2), channel_id=1, replica_groups=mesh['lat_0'=4,'lat_1'=2,'lon_0'=4,'lon_1'=4,'lon_2'=2] {'lon_0','lon_1'..., dimensions={0} | all-to-all | bytes 2097152 | tf_op jit(solution)/shard_map/all_to_all | solution.py:51
  189.5 5.6 %fusion.83 = f32[32,2,1024]{2,1,0:T(2,128)S(1)} fusion(bf16[32,1024,128]{2,1,0:T(8,128)(2,1)} %param.20, bf16[32,2,128]{2,0,1:T(8,128)(2,1)S(1)} %reduce_sum.47), kind=kOutput, calls=%fused_computation.148 | convolution fusion | flops 16777216 | bytes 8667136 | tf_op jit(solution)/shard_map/dot_general | solution.py:187
  195.2 1.6 broadcast_in_dim.10
  196.8 7.1 %all-to-all-start.1 = ((f32[8,32,2,1024]{3,1,2,0:T(8,128)}), f32[8,32,2,1024]{3,1,2,0:T(8,128)S(1)}, u32[]{:S(2)}, u32[]{:S(2)}) async-start(f32[8,32,2,1024]{3,1,2,0:T(8,128)} %broadcast_in_dim.10), calls=%async_computation.1 | async-start | bytes 4194304 | tf_op jit(solution)/shard_map/all_to_all | solution.py:57
  204.0 2.1 cosine_multiply_fusion.1
  206.2 1.8 copy.30
  208.0 2.1 dot_general.16
  210.2 44.3 %all-to-all-done.1 = f32[8,32,2,1024]{3,1,2,0:T(8,128)S(1)} async-done(((f32[8,32,2,1024]{3,1,2,0:T(8,128)}), f32[8,32,2,1024]{3,1,2,0:T(8,128)S(1)}, u32[]{:S(2)}, u32[]{:S(2)}) %all-to-all-start.1) | async-done | bytes 2097184 | tf_op jit(solution)/shard_map/all_to_all | solution.py:57
  254.6 4.6 %fusion.64 = f32[32,2,128]{2,1,0:T(2,128)S(1)} fusion(bf16[32,1024,128]{2,1,0:T(8,128)(2,1)} %param.20, bf16[32,2,1024]{2,0,1:T(8,128)(2,1)S(1)} %multiply_convert_fusion), kind=kOutput, calls=%fused_computation.120 | convolution fusion | flops 16777216 | bytes 8552448 | tf_op jit(solution)/shard_map/dot_general | solution.py:192
  259.2 5.1 %fusion = f32[32,128,128]{2,1,0:T(8,128)} fusion(f32[64,128,1]{1,0,2:T(8,128)S(1)} %bitcast.95, f32[32,128,64]{1,0,2:T(8,128)S(1)} %dot_general.16), kind=kOutput, calls=%fused_computation.2 | convolution fusion | flops 402653184 | bytes 3178496 | tf_op jit(solution)/shard_map/dot_general | solution.py:202
  264.2 5.5 %all-to-all-start.2 = ((f32[32,128,128]{2,1,0:T(8,128)}), f32[32,128,128]{2,1,0:T(8,128)S(1)}, u32[]{:S(2)}, u32[]{:S(2)}) async-start(f32[32,128,128]{2,1,0:T(8,128)} %fusion), calls=%async_computation.2 | async-start | bytes 4194304 | tf_op jit(solution)/shard_map/all_to_all | solution.py:51
  269.9 1.9 fusion.72
  271.8 47.8 %all-to-all-done.2 = f32[32,128,128]{2,1,0:T(8,128)S(1)} async-done(((f32[32,128,128]{2,1,0:T(8,128)}), f32[32,128,128]{2,1,0:T(8,128)S(1)}, u32[]{:S(2)}, u32[]{:S(2)}) %all-to-all-start.2) | async-done | bytes 2097184 | tf_op jit(solution)/shard_map/all_to_all | solution.py:51
  (95 shorter events, 59.0 us)
Async XLA Ops:
  5.7 49.2 %collective-permute-start.1 = (f32[6,8,128]{2,1,0:T(8,128)S(1)}, f32[6,8,128]{2,1,0:T(8,128)S(1)}, u32[]{:S(2)}, u32[]{:S(2)}) collective-permute-start(f32[6,8,128]{2,1,0:T(8,128)S(1)} %get-tuple-element.50), channel_id=1, source_target_pairs={{1,0},{2,1},{3,2},{4,3},{5,4},{6,5},{7,6},{8,7},{9,8},{10,9},{11,1... | collective-permute-start | bytes 73736 | tf_op jit(solution)/shard_map/ppermute | solution.py:31
  9.0 45.9 %collective-permute-start = (f32[6,8,128]{2,1,0:T(8,128)S(1)}, f32[6,8,128]{2,1,0:T(8,128)S(1)}, u32[]{:S(2)}, u32[]{:S(2)}) collective-permute-start(f32[6,8,128]{2,1,0:T(8,128)S(1)} %get-tuple-element.49), channel_id=1, source_target_pairs={{0,1},{1,2},{2,3},{3,4},{4,5},{5,6},{6,7},{7,8},{8,9},{9,10},{10,1... | collective-permute-start | bytes 73736 | tf_op jit(solution)/shard_map/ppermute | solution.py:29
  55.2 20.7 %copy-start.1 = (s32[128,128]{1,0:T(8,128)S(1)}, s32[128,128]{1,0:T(8,128)}, u32[]{:S(2)}) copy-start(s32[128,128]{1,0:T(8,128)} %param.15) | copy-start | bytes 196612
  55.2 14.8 %collective-permute-start.3 = (f32[6,144,8]{2,1,0:T(8,128)S(1)}, f32[6,144,8]{2,1,0:T(8,128)S(1)}, u32[]{:S(2)}, u32[]{:S(2)}) collective-permute-start(f32[6,144,8]{2,1,0:T(8,128)S(1)} %get-tuple-element.48), channel_id=1, source_target_pairs={{32,0},{64,32},{96,64},{128,96},{160,128},{192,160},{224,192},{33,... | collective-permute-start | bytes 82952 | tf_op jit(solution)/shard_map/ppermute | solution.py:31
  56.6 14.8 %collective-permute-start.2 = (f32[6,144,8]{2,1,0:T(8,128)S(1)}, f32[6,144,8]{2,1,0:T(8,128)S(1)}, u32[]{:S(2)}, u32[]{:S(2)}) collective-permute-start(f32[6,144,8]{2,1,0:T(8,128)S(1)} %get-tuple-element.47), channel_id=1, source_target_pairs={{0,32},{32,64},{64,96},{96,128},{128,160},{160,192},{192,224},{1,3... | collective-permute-start | bytes 82952 | tf_op jit(solution)/shard_map/ppermute | solution.py:29
  71.9 4.0 %copy-start = (f32[132,132]{1,0:T(8,128)}, f32[132,132]{1,0:T(8,128)S(1)}, u32[]{:S(2)}) copy-start(f32[132,132]{1,0:T(8,128)S(1)} %get-tuple-element.43) | copy-start | bytes 209092
  72.1 54.3 %copy-start.4 = (s32[8,32]{1,0:T(8,128)S(1)}, s32[8,32]{1,0:T(8,128)}, u32[]{:S(2)}) copy-start(s32[8,32]{1,0:T(8,128)} %param.16) | copy-start | bytes 3076
  76.6 118.5 %copy-start.2 = (f32[128,128]{1,0:T(8,128)}, f32[128,128]{1,0:T(8,128)S(1)}, u32[]{:S(2)}) copy-start(f32[128,128]{1,0:T(8,128)S(1)} %get-tuple-element.5) | copy-start | bytes 196612
  195.1 59.4 %copy-start.3 = (f32[1024]{0:T(1024)S(1)}, f32[1024]{0:T(1024)}, u32[]{:S(2)}) copy-start(f32[1024]{0:T(1024)} %param.21) | copy-start | bytes 12292
  196.8 57.6 %all-to-all-start.1 = ((f32[8,32,2,1024]{3,1,2,0:T(8,128)}), f32[8,32,2,1024]{3,1,2,0:T(8,128)S(1)}, u32[]{:S(2)}, u32[]{:S(2)}) async-start(f32[8,32,2,1024]{3,1,2,0:T(8,128)} %broadcast_in_dim.10), calls=%async_computation.1 | async-start | bytes 4194304 | tf_op jit(solution)/shard_map/all_to_all | solution.py:57
  264.2 55.3 %all-to-all-start.2 = ((f32[32,128,128]{2,1,0:T(8,128)}), f32[32,128,128]{2,1,0:T(8,128)S(1)}, u32[]{:S(2)}, u32[]{:S(2)}) async-start(f32[32,128,128]{2,1,0:T(8,128)} %fusion), calls=%async_computation.2 | async-start | bytes 4194304 | tf_op jit(solution)/shard_map/all_to_all | solution.py:51
where the time goes:
time: 322 us; the launch traced here: 320 us
  blocking collectives  107 us (33%)
  waiting for transfers between devices  98 us (30%)
  other arithmetic  56.1 us (17%)
  starting transfers between devices  26.2 us (8%)
  matrix products  16.3 us (5%)
  local copies, waits for them, and re-layouts  14.1 us (4%)
    psum x5, blocking collectives, one_axis_at_a_time(): value = lax.psum(value, axis)  76.3 us
    all_to_all x1, waiting for transfers between devices, sum_at_owner(): tiles = lax.all_to_all(in_blocks(value, dim, size), axis, 0, 0, tiled=True)  47.8 us
    all_to_all x1, waiting for transfers between devices, from_everyone(): return lax.all_to_all(copies, axis, split_axis=0, concat_axis=0, tiled=True)  44.3 us
    all_to_all x1, blocking collectives, sum_at_owner(): tiles = lax.all_to_all(in_blocks(value, dim, size), axis, 0, 0, tiled=True)  31 us
    cos x16, other arithmetic, potential(): jnp.cos(frequencies[index] * moment + orders[index] * longitude + tide_ph...  21.2 us
    mul x16, other arithmetic, potential(): tide_amp[index] * shape_term  20.3 us
    ppermute x2, starting transfers between devices, padded(): lax.ppermute(tail, axis, [(i, (i + 1) % count) for i in range(ends)])  8.8 us
    all_to_all x1, starting transfers between devices, from_everyone(): return lax.all_to_all(copies, axis, split_axis=0, concat_axis=0, tiled=True)  7.15 us
  transfers between devices with their start and end apart: 6, of which 4 were waited for; matrix products, arithmetic and copies ran while one was open for 17% of the time, Pallas kernels for 0%

commit v1 on v0

--- a/solution.py
+++ b/solution.py
@@ -37,7 +37,7 @@
 
 def one_axis_at_a_time(value, axes):
     for axis in axes:
-        value = lax.psum(value, axis)
+        value = jnp.sum(lax.all_gather(value, axis), axis=0)
     return value
 
 

time: 322 us -> 341 us (1.059)
  other arithmetic: 56.1 us -> 70.5 us
  local copies, waits for them, and re-layouts: 14.1 us -> 25 us
    psum x5 -> x0, blocking collectives: 76.3 us -> none  [one_axis_at_a_time(): value = lax.psum(value, axis)]
    unnamed x0 -> x5, blocking collectives: none -> 72.9 us
    unnamed x14 -> x41, local copies, waits for them, and re-layouts: 3.4 us -> 14.3 us
  transfers between devices with their start and end apart: 6 -> 6, of which waited for: 4 -> 4; matrix products, arithmetic and copies ran while one was open for 17% -> 20% of each run, Pallas kernels for 0% -> 0%
where the time goes in v1:
time: 341 us; the launch traced here: 340 us
  blocking collectives  104 us (30%)
  waiting for transfers between devices  95.3 us (28%)
  other arithmetic  70.5 us (21%)
  starting transfers between devices  26.2 us (8%)
  local copies, waits for them, and re-layouts  25 us (7%)
  matrix products  16.2 us (5%)
    unnamed x5, blocking collectives  72.9 us
    all_to_all x1, waiting for transfers between devices, sum_at_owner(): tiles = lax.all_to_all(in_blocks(value, dim, size), axis, 0, 0, tiled=True)  47.8 us
    all_to_all x1, waiting for transfers between devices, from_everyone(): return lax.all_to_all(copies, axis, split_axis=0, concat_axis=0, tiled=True)  44.2 us
    all_to_all x1, blocking collectives, sum_at_owner(): tiles = lax.all_to_all(in_blocks(value, dim, size), axis, 0, 0, tiled=True)  31 us
    cos x16, other arithmetic, potential(): jnp.cos(frequencies[index] * moment + orders[index] * longitude + tide_ph...  23.6 us
    mul x16, other arithmetic, potential(): tide_amp[index] * shape_term  23.1 us
    unnamed x41, local copies, waits for them, and re-layouts  14.3 us
    ppermute x2, starting transfers between devices, padded(): lax.ppermute(tail, axis, [(i, (i + 1) % count) for i in range(ends)])  8.8 us
  transfers between devices with their start and end apart: 6, of which 4 were waited for; matrix products, arithmetic and copies ran while one was open for 20% of the time, Pallas kernels for 0%

profile of v1, /device:TPU:1, one launch (start us, length us, event | category | flops | bytes accessed | tf_op | source)
XLA Modules:
  0.0 339.5 jit_solution(10638622199405386326)
XLA Ops:
  5.7 3.3 collective-permute-start.1
  17.9 1.9 broadcast_multiply_fusion.10
  21.2 1.9 add_cosine_fusion.10
  27.6 1.9 add_cosine_fusion.12
  30.8 1.9 broadcast_multiply_fusion.15
  34.1 1.9 add_cosine_fusion.14
  60.8 2.1 cosine_multiply_fusion
  67.4 8.8 %collective-permute-start.2 = (f32[6,144,8]{2,1,0:T(8,128)S(1)}, f32[6,144,8]{2,1,0:T(8,128)S(1)}, u32[]{:S(2)}, u32[]{:S(2)}) collective-permute-start(f32[6,144,8]{2,1,0:T(8,128)S(1)} %get-tuple-element.47), channel_id=1, source_target_pairs={{0,32},{32,64},{64,96},{96,128},{128,160},{160,192},{192,224},{1,3... | collective-permute-start | bytes 82952 | tf_op jit(solution)/shard_map/ppermute | solution.py:29
  78.9 1.9 collective-permute-done.3
  91.5 27.2 %all-reduce = f32[4]{0:T(128)S(1)} all-reduce(f32[4]{0:T(128)S(1)} %dynamic-update-slice), channel_id=1, replica_groups=mesh['lat_0'=4,'lat_1'=2,'lon_0'=4,'lon_1'=4,'lon_2'=2] {'lat_0'}, use_global_device_ids=true, to_apply=%add | all-reduce | flops 4 | bytes 32
  121.3 7.9 %all-reduce.1 = f32[2]{0:T(128)S(1)} all-reduce(f32[2]{0:T(128)S(1)} %dynamic-update-slice.1), channel_id=1, replica_groups=mesh['lat_0'=4,'lat_1'=2,'lon_0'=4,'lon_1'=4,'lon_2'=2] {'lat_1'}, use_global_device_ids=true, to_apply=%add.1 | all-reduce | flops 2 | bytes 16
  131.8 10.6 %all-reduce.2 = f32[4]{0:T(128)S(1)} all-reduce(f32[4]{0:T(128)S(1)} %dynamic-update-slice.2), channel_id=1, replica_groups=mesh['lat_0'=4,'lat_1'=2,'lon_0'=4,'lon_1'=4,'lon_2'=2] {'lon_0'}, use_global_device_ids=true, to_apply=%add.2 | all-reduce | flops 4 | bytes 32
  145.0 17.6 %all-reduce.3 = f32[4]{0:T(128)S(1)} all-reduce(f32[4]{0:T(128)S(1)} %dynamic-update-slice.3), channel_id=1, replica_groups=mesh['lat_0'=4,'lat_1'=2,'lon_0'=4,'lon_1'=4,'lon_2'=2] {'lon_1'}, use_global_device_ids=true, to_apply=%add.3 | all-reduce | flops 4 | bytes 32
  165.2 9.5 %all-reduce.4 = f32[2]{0:T(128)S(1)} all-reduce(f32[2]{0:T(128)S(1)} %dynamic-update-slice.4), channel_id=1, replica_groups=mesh['lat_0'=4,'lat_1'=2,'lon_0'=4,'lon_1'=4,'lon_2'=2] {'lon_2'}, use_global_device_ids=true, to_apply=%add.4 | all-reduce | flops 2 | bytes 16
  177.7 31.0 %all_to_all.15 = f32[32,32,2,128]{3,1,2,0:T(8,128)S(1)} all-to-all(f32[32,32,2,128]{3,1,2,0:T(8,128)S(1)} %fusion.2), channel_id=1, replica_groups=mesh['lat_0'=4,'lat_1'=2,'lon_0'=4,'lon_1'=4,'lon_2'=2] {'lon_0','lon_1'..., dimensions={0} | all-to-all | bytes 2097152 | tf_op jit(solution)/shard_map/all_to_all | solution.py:51
  208.7 5.6 %fusion.83 = f32[32,2,1024]{2,1,0:T(2,128)S(1)} fusion(bf16[32,1024,128]{2,1,0:T(8,128)(2,1)} %param.20, bf16[32,2,128]{2,0,1:T(8,128)(2,1)S(1)} %reduce_sum.97), kind=kOutput, calls=%fused_computation.148 | convolution fusion | flops 16777216 | bytes 8667136 | tf_op jit(solution)/shard_map/dot_general | solution.py:187
  216.1 7.1 %all-to-all-start.1 = ((f32[8,32,2,1024]{3,1,2,0:T(8,128)}), f32[8,32,2,1024]{3,1,2,0:T(8,128)S(1)}, u32[]{:S(2)}, u32[]{:S(2)}) async-start(f32[8,32,2,1024]{3,1,2,0:T(8,128)} %broadcast_in_dim.10), calls=%async_computation.1 | async-start | bytes 4194304 | tf_op jit(solution)/shard_map/all_to_all | solution.py:57
  223.2 2.1 cosine_multiply_fusion.1
  227.3 2.1 dot_general.16
  229.4 44.2 %all-to-all-done.1 = f32[8,32,2,1024]{3,1,2,0:T(8,128)S(1)} async-done(((f32[8,32,2,1024]{3,1,2,0:T(8,128)}), f32[8,32,2,1024]{3,1,2,0:T(8,128)S(1)}, u32[]{:S(2)}, u32[]{:S(2)}) %all-to-all-start.1) | async-done | bytes 2097184 | tf_op jit(solution)/shard_map/all_to_all | solution.py:57
  273.8 4.6 %fusion.64 = f32[32,2,128]{2,1,0:T(2,128)S(1)} fusion(bf16[32,1024,128]{2,1,0:T(8,128)(2,1)} %param.20, bf16[32,2,1024]{2,0,1:T(8,128)(2,1)S(1)} %multiply_convert_fusion), kind=kOutput, calls=%fused_computation.120 | convolution fusion | flops 16777216 | bytes 8552448 | tf_op jit(solution)/shard_map/dot_general | solution.py:192
  278.4 5.1 %fusion = f32[32,128,128]{2,1,0:T(8,128)} fusion(f32[64,128,1]{1,0,2:T(8,128)S(1)} %bitcast.105, f32[32,128,64]{1,0,2:T(8,128)S(1)} %dot_general.16), kind=kOutput, calls=%fused_computation.2 | convolution fusion | flops 402653184 | bytes 3178496 | tf_op jit(solution)/shard_map/dot_general | solution.py:202
  283.4 5.6 %all-to-all-start.2 = ((f32[32,128,128]{2,1,0:T(8,128)}), f32[32,128,128]{2,1,0:T(8,128)S(1)}, u32[]{:S(2)}, u32[]{:S(2)}) async-start(f32[32,128,128]{2,1,0:T(8,128)} %fusion), calls=%async_computation.2 | async-start | bytes 4194304 | tf_op jit(solution)/shard_map/all_to_all | solution.py:51
  291.0 47.8 %all-to-all-done.2 = f32[32,128,128]{2,1,0:T(8,128)S(1)} async-done(((f32[32,128,128]{2,1,0:T(8,128)}), f32[32,128,128]{2,1,0:T(8,128)S(1)}, u32[]{:S(2)}, u32[]{:S(2)}) %all-to-all-start.2) | async-done | bytes 2097184 | tf_op jit(solution)/shard_map/all_to_all | solution.py:51
  (127 shorter events, 83.3 us)
Async XLA Ops:
  5.7 60.0 %collective-permute-start.1 = (f32[6,8,128]{2,1,0:T(8,128)S(1)}, f32[6,8,128]{2,1,0:T(8,128)S(1)}, u32[]{:S(2)}, u32[]{:S(2)}) collective-permute-start(f32[6,8,128]{2,1,0:T(8,128)S(1)} %get-tuple-element.50), channel_id=1, source_target_pairs={{1,0},{2,1},{3,2},{4,3},{5,4},{6,5},{7,6},{8,7},{9,8},{10,9},{11,1... | collective-permute-start | bytes 73736 | tf_op jit(solution)/shard_map/ppermute | solution.py:31
  9.0 56.7 %collective-permute-start = (f32[6,8,128]{2,1,0:T(8,128)S(1)}, f32[6,8,128]{2,1,0:T(8,128)S(1)}, u32[]{:S(2)}, u32[]{:S(2)}) collective-permute-start(f32[6,8,128]{2,1,0:T(8,128)S(1)} %get-tuple-element.49), channel_id=1, source_target_pairs={{0,1},{1,2},{2,3},{3,4},{4,5},{5,6},{6,7},{7,8},{8,9},{9,10},{10,1... | collective-permute-start | bytes 73736 | tf_op jit(solution)/shard_map/ppermute | solution.py:29
  66.0 22.8 %copy-start.1 = (s32[128,128]{1,0:T(8,128)S(1)}, s32[128,128]{1,0:T(8,128)}, u32[]{:S(2)}) copy-start(s32[128,128]{1,0:T(8,128)} %param.15) | copy-start | bytes 196612
  66.0 14.8 %collective-permute-start.3 = (f32[6,144,8]{2,1,0:T(8,128)S(1)}, f32[6,144,8]{2,1,0:T(8,128)S(1)}, u32[]{:S(2)}, u32[]{:S(2)}) collective-permute-start(f32[6,144,8]{2,1,0:T(8,128)S(1)} %get-tuple-element.48), channel_id=1, source_target_pairs={{32,0},{64,32},{96,64},{128,96},{160,128},{192,160},{224,192},{33,... | collective-permute-start | bytes 82952 | tf_op jit(solution)/shard_map/ppermute | solution.py:31
  67.4 14.8 %collective-permute-start.2 = (f32[6,144,8]{2,1,0:T(8,128)S(1)}, f32[6,144,8]{2,1,0:T(8,128)S(1)}, u32[]{:S(2)}, u32[]{:S(2)}) collective-permute-start(f32[6,144,8]{2,1,0:T(8,128)S(1)} %get-tuple-element.47), channel_id=1, source_target_pairs={{0,32},{32,64},{64,96},{96,128},{128,160},{160,192},{192,224},{1,3... | collective-permute-start | bytes 82952 | tf_op jit(solution)/shard_map/ppermute | solution.py:29
  77.5 6.9 %copy-start.4 = (f32[136]{0:T(256)S(1)}, f32[136]{0:T(256)}, u32[]{:S(2)}) copy-start(f32[136]{0:T(256)} %get-tuple-element.55) | copy-start | bytes 1636
  77.5 6.9 %copy-start.5 = (f32[136]{0:T(256)S(1)}, f32[136]{0:T(256)}, u32[]{:S(2)}) copy-start(f32[136]{0:T(256)} %get-tuple-element.56) | copy-start | bytes 1636
  77.5 6.9 %copy-start.6 = (f32[136]{0:T(256)S(1)}, f32[136]{0:T(256)}, u32[]{:S(2)}) copy-start(f32[136]{0:T(256)} %get-tuple-element.114) | copy-start | bytes 1636
  80.8 10.1 %copy-start.10 = (u32[256]{0:T(256)S(1)}, u32[256]{0:T(256)}, u32[]{:S(2)}) copy-start(u32[256]{0:T(256)} %constant.358) | copy-start | bytes 3076
  80.8 39.9 %copy-start.9 = (u32[256]{0:T(256)S(1)}, u32[256]{0:T(256)}, u32[]{:S(2)}) copy-start(u32[256]{0:T(256)} %constant.363) | copy-start | bytes 3076
  80.8 50.4 %copy-start.8 = (u32[256]{0:T(256)S(1)}, u32[256]{0:T(256)}, u32[]{:S(2)}) copy-start(u32[256]{0:T(256)} %constant.368) | copy-start | bytes 3076
  80.8 63.6 %copy-start.7 = (u32[256]{0:T(256)S(1)}, u32[256]{0:T(256)}, u32[]{:S(2)}) copy-start(u32[256]{0:T(256)} %constant.373) | copy-start | bytes 3076
  82.7 80.5 %copy-start = (f32[132,132]{1,0:T(8,128)}, f32[132,132]{1,0:T(8,128)S(1)}, u32[]{:S(2)}) copy-start(f32[132,132]{1,0:T(8,128)S(1)} %get-tuple-element.43) | copy-start | bytes 209092
  89.5 126.6 %copy-start.2 = (f32[128,128]{1,0:T(8,128)}, f32[128,128]{1,0:T(8,128)S(1)}, u32[]{:S(2)}) copy-start(f32[128,128]{1,0:T(8,128)S(1)} %get-tuple-element.5) | copy-start | bytes 196612
  214.3 59.4 %copy-start.3 = (f32[1024]{0:T(1024)S(1)}, f32[1024]{0:T(1024)}, u32[]{:S(2)}) copy-start(f32[1024]{0:T(1024)} %param.21) | copy-start | bytes 12292
  216.1 57.6 %all-to-all-start.1 = ((f32[8,32,2,1024]{3,1,2,0:T(8,128)}), f32[8,32,2,1024]{3,1,2,0:T(8,128)S(1)}, u32[]{:S(2)}, u32[]{:S(2)}) async-start(f32[8,32,2,1024]{3,1,2,0:T(8,128)} %broadcast_in_dim.10), calls=%async_computation.1 | async-start | bytes 4194304 | tf_op jit(solution)/shard_map/all_to_all | solution.py:57
  283.4 55.3 %all-to-all-start.2 = ((f32[32,128,128]{2,1,0:T(8,128)}), f32[32,128,128]{2,1,0:T(8,128)S(1)}, u32[]{:S(2)}, u32[]{:S(2)}) async-start(f32[32,128,128]{2,1,0:T(8,128)} %fusion), calls=%async_computation.2 | async-start | bytes 4194304 | tf_op jit(solution)/shard_map/all_to_all | solution.py:51
